TPU v7x, 32 devices: a whole 2x2x4 slice. The times are simulated.
32 devices in a mesh: seq: 8 (over y, x, core), head: 4 (over z).
Axes of the slice: x: 2, y: 2, z: 4, core: 2. Of those that a mesh axis runs over, the one named last changes fastest.
Arguments:
- frames: bfloat16 [8192, 1024], P(('seq', 'head')), may hold values from -6 to 6
- cotangent: bfloat16 [8192, 1024], P(('seq', 'head')), may hold values from -6 to 6
- norm_gain: float32 [1024], replicated, may hold values from 0.25 to 1.75
- w_qkv: bfloat16 [3, 1024, 1024], replicated
- w_out: bfloat16 [1024, 1024], replicated, may hold values from -0.1875 to 0.1875
Outputs:
- output: bfloat16 [8192, 1024], P(('seq', 'head'))
- grad_frames: bfloat16 [8192, 1024], P(('seq', 'head'))
- grad_qkv: float32 [3, 1024, 1024], P(None, 'seq', 'head')
- grad_out: float32 [1024, 1024], P('seq', 'head')
All inputs are finite; a program needn't handle non-finite values.
Results may differ from a plain program's by a relative error of at most 0.015.
Values may be sent and summed in bfloat16 or wider, within the bound.
A program may use at most 128 MiB of HBM per device.

v0:
```python
import jax
import jax.numpy as jnp
from jax import lax
from jax.sharding import PartitionSpec as P

HEAD_SIZE = 128
WINDOW = 128
EPSILON = 1e-05
MASKED = -1e30


def with_halo(shard, sides, width):
    for axis, dim in sides:
        devices, length = (lax.axis_size(axis), shard.shape[dim])
        up = [(i, (i + 1) % devices) for i in range(devices - 1)]
        down = [(j, i) for i, j in up]
        last = lax.slice_in_dim(shard, length - width, length, axis=dim)
        first = lax.slice_in_dim(shard, 0, width, axis=dim)
        before = lax.ppermute(last, axis, up)
        after = lax.ppermute(first, axis, down)
        shard = jnp.concatenate([before, shard, after], axis=dim)
    return shard


def layer_norm(values, norm_gain):
    average = jnp.mean(values, axis=-1, keepdims=True)
    centered = values - average
    variance = jnp.mean(centered * centered, axis=-1, keepdims=True)
    return centered * lax.rsqrt(variance + EPSILON) * norm_gain


def norm_grad(frames, norm_gain, upstream):
    _, pullback = jax.vjp(lambda v: layer_norm(v, norm_gain), frames.astype(jnp.float32))
    return pullback(upstream.astype(jnp.float32))[0]


def attention(query_rows, key_rows, value_rows, offset, frame_total):
    length, channels = query_rows.shape
    head_count = channels // HEAD_SIZE
    block_rows = min(length, 512)
    block_count = length // block_rows
    key_span = block_rows + 2 * WINDOW
    score_scale = HEAD_SIZE ** (-0.5)

    def one_block(block_index):
        anchor = block_index * block_rows
        query_part = lax.dynamic_slice_in_dim(query_rows, anchor, block_rows, 0).reshape(
            block_rows, head_count, HEAD_SIZE
        )
        key_part = lax.dynamic_slice_in_dim(key_rows, anchor, key_span, 0).reshape(
            key_span, head_count, HEAD_SIZE
        )
        value_part = lax.dynamic_slice_in_dim(value_rows, anchor, key_span, 0).reshape(
            key_span, head_count, HEAD_SIZE
        )
        query_pos = offset + anchor + jnp.arange(block_rows, dtype=jnp.int32)
        key_pos = offset + anchor - WINDOW + jnp.arange(key_span, dtype=jnp.int32)
        distance = query_pos[:, None] - key_pos[None, :]
        allowed = (
            (jnp.abs(distance) <= WINDOW)
            & (key_pos >= 0)[None, :]
            & (key_pos < frame_total)[None, :]
        )
        scores = (
            jnp.einsum("qhe,khe->hqk", query_part, key_part, precision=lax.Precision.HIGHEST)
            * score_scale
        )
        scores = jnp.where(allowed[None], scores, MASKED)
        row_max = lax.stop_gradient(jnp.max(scores, axis=-1, keepdims=True))
        weights = jnp.exp(scores - row_max)
        weights = weights / jnp.sum(weights, axis=-1, keepdims=True)
        combined = jnp.einsum("hqk,khe->qhe", weights, value_part, precision=lax.Precision.HIGHEST)
        return combined.reshape(block_rows, channels)

    results = lax.map(jax.checkpoint(one_block), jnp.arange(block_count, dtype=jnp.int32))
    return results.reshape(length, channels)


def attention_grad(query_rows, key_rows, value_rows, offset, frame_total, upstream):
    _, pullback = jax.vjp(
        lambda a, b, c: attention(a, b, c, offset, frame_total), query_rows, key_rows, value_rows
    )
    return pullback(upstream.astype(jnp.float32))


def to_heads(stacked):
    return lax.all_to_all(stacked, "head", split_axis=2, concat_axis=1, tiled=True)


def to_time(stacked):
    return lax.all_to_all(stacked, "head", split_axis=1, concat_axis=2, tiled=True)


def sum_columns(term):
    return lax.psum_scatter(
        term.astype(jnp.bfloat16), "head", scatter_dimension=2, tiled=True
    ).astype(jnp.float32)


def sum_rows(term):
    return lax.psum_scatter(
        term.astype(jnp.bfloat16), "seq", scatter_dimension=1, tiled=True
    ).astype(jnp.float32)


def shards(frames, cotangent, norm_gain, w_qkv, w_out):
    frame_rows = frames.shape[0]
    head_groups = lax.axis_size("head")
    frame_total = lax.axis_size("seq") * head_groups * frame_rows
    grad_scale = frame_total ** (-0.5)
    normed = layer_norm(frames.astype(jnp.float32), norm_gain).astype(jnp.bfloat16)
    projected = jnp.einsum("td,cdf->ctf", normed, w_qkv, preferred_element_type=jnp.float32).astype(
        jnp.bfloat16
    )
    offset = lax.axis_index("seq") * (head_groups * frame_rows)
    local_qkv = to_heads(projected)
    bordered = with_halo(local_qkv[1:], (("seq", 1),), WINDOW)
    query_rows = local_qkv[0].astype(jnp.float32)
    key_rows = bordered[0].astype(jnp.float32)
    value_rows = bordered[1].astype(jnp.float32)
    length = query_rows.shape[0]
    attended = attention(query_rows, key_rows, value_rows, offset, frame_total).astype(jnp.bfloat16)
    mixed_rows = to_time(attended[None])[0]
    output = (
        frames.astype(jnp.float32) + jnp.dot(mixed_rows, w_out, preferred_element_type=jnp.float32)
    ).astype(jnp.bfloat16)
    grad_mixed = jnp.einsum(
        "tf,df->td", cotangent, w_out, preferred_element_type=jnp.float32
    ).astype(jnp.bfloat16)
    grad_attended = to_heads(grad_mixed[None])[0]
    grad_query, grad_keys, grad_values = attention_grad(
        query_rows, key_rows, value_rows, offset, frame_total, grad_attended
    )
    pair_grads = jnp.stack([grad_keys, grad_values])
    edge_grads = jnp.concatenate([pair_grads[:, :WINDOW], pair_grads[:, length + WINDOW :]], axis=1)
    returned = with_halo(edge_grads.astype(jnp.bfloat16), (("seq", 1),), WINDOW).astype(
        edge_grads.dtype
    )
    interior = pair_grads[:, WINDOW : length + WINDOW]
    interior = interior.at[:, :WINDOW].add(returned[:, :WINDOW])
    interior = interior.at[:, length - WINDOW :].add(returned[:, 3 * WINDOW :])
    grad_local = jnp.concatenate([grad_query[None], interior], axis=0).astype(jnp.bfloat16)
    grad_time = to_time(grad_local)
    grad_normed = jnp.einsum(
        "ctf,cdf->td", grad_time, w_qkv, preferred_element_type=jnp.float32
    ).astype(jnp.bfloat16)
    grad_frames = (
        cotangent.astype(jnp.float32) + norm_grad(frames, norm_gain, grad_normed)
    ).astype(jnp.bfloat16)
    out_term = (
        jnp.einsum("td,tf->df", mixed_rows, cotangent, preferred_element_type=jnp.float32)[None]
        * grad_scale
    )
    grad_out = sum_rows(sum_columns(out_term))[0]
    time_term = (
        jnp.einsum("td,ctf->cdf", normed, grad_time, preferred_element_type=jnp.float32)
        * grad_scale
    )
    grad_qkv = sum_rows(sum_columns(time_term))
    return (output, grad_frames, grad_qkv, grad_out)


def solution(mesh):
    in_specs = (P(("seq", "head"), None), P(("seq", "head"), None), P(), P(), P())
    out_specs = (
        P(("seq", "head"), None),
        P(("seq", "head"), None),
        P(None, "seq", "head"),
        P("seq", "head"),
    )
    return jax.shard_map(shards, mesh=mesh, in_specs=in_specs, out_specs=out_specs, check_vma=False)
```

profile of v0, /device:TPU:0, one launch (start us, length us, event | category | flops | bytes accessed | tf_op | source)
XLA Modules:
  0.0 544.6 jit_solution(4253332027485808211)
XLA Ops:
  13.1 4.8 reduce.5
  18.9 6.3 %all-to-all-start.2 = ((bf16[4,2,32768]{2,1,0:T(2,128)(2,1)}), bf16[4,2,32768]{2,1,0:T(2,128)(2,1)S(1)}, u32[]{:S(2)}, u32[]{:S(2)}) async-start(bf16[4,2,32768]{2,1,0:T(2,128)(2,1)} %reshape.388), calls=%async_computation.2 | async-start | bytes 1048576 | tf_op jit(solution)/shard_map/all_to_all | solution.py:87
  26.8 5.9 %fusion.34 = bf16[3,256,1024]{2,1,0:T(8,128)(2,1)} fusion(bf16[3,1024,1024]{2,1,0:T(8,128)(2,1)} %param.16, bf16[256,1024]{1,0:T(8,128)(2,1)S(1)} %copy-done.13, f32[1024]{0:T(1024)S(1)} %copy-done.28, f32[256]{0:T(256)S(1)} %fusion.53, f32[256]{0:T(256)S(1)} %broadcast_multiply_fusion), kind=kOutput, calls=%fused_computation.76 | convolution fusion | flops 1612709888 | bytes 8394752 | tf_op jit(solution)/shard_map/td,cdf->ctf/dot_general | solution.py:112
  32.6 4.1 copy.107
  39.7 4.5 all-to-all-start
  47.9 44.0 %all-to-all-done = bf16[3,256,1024]{1,0,2:T(4,128)(2,1)} async-done(((bf16[3,256,1024]{1,0,2:T(4,128)(2,1)}), bf16[3,256,1024]{1,0,2:T(4,128)(2,1)}, u32[]{:S(2)}, u32[]{:S(2)}) %all-to-all-start) | async-done | bytes 1572896 | tf_op jit(solution)/shard_map/all_to_all | solution.py:87
  92.0 4.1 copy.109
  111.7 29.2 %while.32 = (s32[]{:T(128)}, bf16[2,512,256]{2,1,0:T(8,128)(2,1)}, s32[2]{0:T(128)S(1)}, f32[1280,256]{0,1:T(8,128)}, s32[]{:T(128)}, /*index=5*/f32[1024,256]{0...) while((s32[]{:T(128)}, bf16[2,512,256]{2,1,0:T(8,128)(2,1)}, ...), condition=%wide.region_5.6_spmd, body=%wide.region_2.5_spmd.sunk | while | flops 2426537472 | bytes 25986388 | solution.py:75
  121.3 4.1 fusion.116
  135.9 4.1 fusion.116
  142.8 4.7 reduce.4
  149.4 4.1 all-to-all-start.1
  157.0 70.9 %while.33 = (s32[]{:T(128)}, f32[1024,256]{1,0:T(8,128)}, f32[1280,256]{0,1:T(8,128)}, f32[1280,256]{0,1:T(8,128)}, s32[2]{0:T(128)S(1)}, /*index=5*/f32[2,512,2...) while((s32[]{:T(128)}, f32[1024,256]{1,0:T(8,128)}, ...), condition=%wide.region_10.11_spmd, body=%wide.region_6.10_spmd.sunk | while | flops 6061953024 | bytes 89728512 | solution.py:75
  208.9 3.9 multiply_reduce_fusion.2
  227.9 3.9 copy.138
  241.7 4.1 fusion.27
  245.9 4.8 collective-permute-start.2
  258.9 74.3 %all_to_all.57 = bf16[3,1024,256]{2,0,1:T(4,128)(2,1)S(1)} all-to-all(bf16[3,1024,256]{2,0,1:T(4,128)(2,1)S(1)} %pad_maximum_fusion.1), channel_id=1, replica_groups=mesh['seq'=8,'head'=4] {'head'}, dimensions={1} | all-to-all | bytes 3145728 | tf_op jit(solution)/shard_map/all_to_all | solution.py:91
  339.7 6.1 %fusion.26 = bf16[3,1024,1024]{1,2,0:T(8,128)(2,1)} fusion(bf16[3,256,1024]{2,1,0:T(8,128)(2,1)} %all_to_all.52, bf16[256,1024]{1,0:T(8,128)(2,1)S(1)} %copy-done.14, f32[1024]{0:T(1024)S(1)} %copy-done.29, f32[256]{0:T(256)S(1)} %copy-done.25, f32[256]{0:T(256)S(1)} %copy-done.23), kind=kOutput, calls=%fused_computation.55 | convolution fusion | flops 1618214912 | bytes 8394752 | tf_op jit(solution)/shard_map/td,ctf->cdf/dot_general | solution.py:156
  346.6 109.6 %reduce-scatter.7.cloned.1.call-done = bf16[3,1024,256]{1,2,0:T(8,128)(2,1)} async-done(((bf16[3,1024,1024]{1,2,0:T(8,128)(2,1)}), bf16[3,1024,256]{1,2,0:T(8,128)(2,1)}) %reduce-scatter.7.cloned.1.call-update) | async-done | bytes 1572880 | tf_op jit(solution)/shard_map/reduce_scatter | solution.py:95
  456.2 4.4 copy.140
  465.3 5.1 fusion.43
  472.0 21.9 %reduce-scatter.11.cloned.1.call-done = bf16[1,128,256]{2,1,0:T(8,128)(2,1)} async-done(((bf16[1,1024,256]{2,1,0:T(8,128)(2,1)}), bf16[1,128,256]{2,1,0:T(8,128)(2,1)}) %reduce-scatter.11.cloned.1.call-update) | async-done | bytes 65552 | tf_op jit(solution)/shard_map/reduce_scatter | solution.py:101
  495.5 40.1 %reduce-scatter.13.cloned.1.call-done = bf16[128,768]{1,0:T(8,128)(2,1)} async-done(((bf16[1024,768]{1,0:T(8,128)(2,1)}), bf16[128,768]{1,0:T(8,128)(2,1)}) %reduce-scatter.13.cloned.1.call-update) | async-done | bytes 196624
  (224 shorter events, 145.9 us)
Async XLA Ops:
  10.5 14.7 %copy-start.13 = (bf16[256,1024]{1,0:T(8,128)(2,1)S(1)}, bf16[256,1024]{1,0:T(8,128)(2,1)}, u32[]{:S(2)}) copy-start(bf16[256,1024]{1,0:T(8,128)(2,1)} %param.13) | copy-start | bytes 1572868
  10.6 16.2 %copy-start.28 = (f32[1024]{0:T(1024)S(1)}, f32[1024]{0:T(1024)}, u32[]{:S(2)}) copy-start(f32[1024]{0:T(1024)} %param.15) | copy-start | bytes 12292
  18.9 20.8 %all-to-all-start.2 = ((bf16[4,2,32768]{2,1,0:T(2,128)(2,1)}), bf16[4,2,32768]{2,1,0:T(2,128)(2,1)S(1)}, u32[]{:S(2)}, u32[]{:S(2)}) async-start(bf16[4,2,32768]{2,1,0:T(2,128)(2,1)} %reshape.388), calls=%async_computation.2 | async-start | bytes 1048576 | tf_op jit(solution)/shard_map/all_to_all | solution.py:87
  39.7 4.5 copy-start.17
  39.7 52.3 %all-to-all-start = ((bf16[3,256,1024]{1,0,2:T(4,128)(2,1)}), bf16[3,256,1024]{1,0,2:T(4,128)(2,1)}, u32[]{:S(2)}, u32[]{:S(2)}) async-start(bf16[3,256,1024]{1,0,2:T(4,128)(2,1)} %copy.107), calls=%async_computation | async-start | bytes 4194304 | tf_op jit(solution)/shard_map/all_to_all | solution.py:87
  102.4 7.5 %collective-permute-start = (bf16[2,128,256]{1,2,0:T(8,128)(2,1)}, bf16[2,128,256]{1,2,0:T(8,128)(2,1)S(1)}, u32[]{:S(2)}, u32[]{:S(2)}) collective-permute-start(bf16[2,128,256]{1,2,0:T(8,128)(2,1)} %get-tuple-element.473), channel_id=1, source_target_pairs={{0,4},{4,8},{8,12},{12,16},{16,20},{20,24},{24,28},{1,5},{5,9},{9,... | collective-permute-start | bytes 393224 | tf_op jit(solution)/shard_map/ppermute | solution.py:19
  103.7 6.2 %collective-permute-start.1 = (bf16[2,128,256]{1,2,0:T(8,128)(2,1)S(1)}, bf16[2,128,256]{1,2,0:T(8,128)(2,1)S(1)}, u32[]{:S(2)}, u32[]{:S(2)}) collective-permute-start(bf16[2,128,256]{1,2,0:T(8,128)(2,1)S(1)} %get-tuple-element.474), channel_id=1, source_target_pairs={{4,0},{8,4},{12,8},{16,12},{20,16},{24,20},{28,24},{5,1},{9,5},{13... | collective-permute-start | bytes 393224 | tf_op jit(solution)/shard_map/ppermute | solution.py:20
  135.9 4.2 copy-start.20
  149.4 84.5 %all-to-all-start.1 = ((bf16[4,2,32768]{2,1,0:T(2,128)(2,1)}), bf16[4,2,32768]{2,1,0:T(2,128)(2,1)}, u32[]{:S(2)}, u32[]{:S(2)}) async-start(bf16[4,2,32768]{2,1,0:T(2,128)(2,1)} %reshape.390), calls=%async_computation.1 | async-start | bytes 1048576 | tf_op jit(solution)/shard_map/all_to_all | solution.py:91
  153.6 192.3 %reduce-scatter.9.cloned.1.call-start = ((), (), s32[]{:S(2)}) async-start(), calls=%async_computation.9 | async-start | bytes 2621440 | tf_op jit(solution)/shard_map/reduce_scatter | solution.py:95
  241.6 10.4 %copy-start.9 = (f32[1024,256]{1,0:T(8,128)S(1)}, f32[1024,256]{1,0:T(8,128)}, u32[]{:S(2)}) copy-start(f32[1024,256]{1,0:T(8,128)} %get-tuple-element.325) | copy-start | bytes 3145732
  241.6 214.6 %reduce-scatter.7.cloned.1.call-start = ((), (), s32[]{:S(2)}) async-start(), calls=%async_computation.8 | async-start | bytes 7864320 | tf_op jit(solution)/shard_map/reduce_scatter | solution.py:95
  241.7 11.2 %copy-start.10 = (f32[1,1280,256]{2,0,1:T(1,128)S(1)}, f32[1,1280,256]{2,0,1:T(1,128)}, u32[]{:S(2)}) copy-start(f32[1,1280,256]{2,0,1:T(1,128)} %copy.138) | copy-start | bytes 3932164
  241.7 11.2 %copy-start.11 = (f32[1,1280,256]{2,0,1:T(1,128)S(1)}, f32[1,1280,256]{2,0,1:T(1,128)}, u32[]{:S(2)}) copy-start(f32[1,1280,256]{2,0,1:T(1,128)} %copy.139) | copy-start | bytes 3932164
  245.9 8.9 %collective-permute-start.2 = (bf16[2,128,256]{2,0,1:T(2,128)(2,1)S(1)}, bf16[2,128,256]{2,0,1:T(2,128)(2,1)S(1)}, u32[]{:S(2)}, u32[]{:S(2)}) collective-permute-start(bf16[2,128,256]{2,0,1:T(2,128)(2,1)S(1)} %get-tuple-element.469), channel_id=1, source_target_pairs={{0,4},{4,8},{8,12},{12,16},{16,20},{20,24},{24,28},{1,5},{5,9},{9,... | collective-permute-start | bytes 393224 | tf_op jit(solution)/shard_map/ppermute | solution.py:19
  250.7 4.5 collective-permute-start.3
  333.2 6.5 %copy-start.14 = (bf16[256,1024]{1,0:T(8,128)(2,1)S(1)}, bf16[256,1024]{1,0:T(8,128)(2,1)}, u32[]{:S(2)}) copy-start(bf16[256,1024]{1,0:T(8,128)(2,1)} %param.13) | copy-start | bytes 1572868
  333.2 6.5 %copy-start.23 = (f32[256]{0:T(256)S(1)}, f32[256]{0:T(256)}, u32[]{:S(2)}) copy-start(f32[256]{0:T(256)} %copy-done.22) | copy-start | bytes 3076
  333.2 6.5 %copy-start.25 = (f32[256]{0:T(256)S(1)}, f32[256]{0:T(256)}, u32[]{:S(2)}) copy-start(f32[256]{0:T(256)} %copy-done.24) | copy-start | bytes 3076
  333.2 6.5 %copy-start.29 = (f32[1024]{0:T(1024)S(1)}, f32[1024]{0:T(1024)}, u32[]{:S(2)}) copy-start(f32[1024]{0:T(1024)} %param.15) | copy-start | bytes 12292
  345.8 148.2 %reduce-scatter.11.cloned.1.call-start = ((), (), s32[]{:S(2)}) async-start(), calls=%async_computation.10 | async-start | bytes 589824 | tf_op jit(solution)/shard_map/reduce_scatter | solution.py:101
  346.5 189.0 %reduce-scatter.13.cloned.1.call-start = ((), (), s32[]{:S(2)}) async-start(), calls=%async_computation.11 | async-start | bytes 1769472
  465.3 5.1 copy-start.27
  465.3 5.5 %copy-start.18 = (bf16[256,1024]{1,0:T(8,128)(2,1)S(1)}, bf16[256,1024]{1,0:T(8,128)(2,1)}, u32[]{:S(2)}) copy-start(bf16[256,1024]{1,0:T(8,128)(2,1)} %param.14) | copy-start | bytes 1572868
  (27 other events, 72.0 us)
Sparse Core Ops, SparseCore 0:
  241.7 66.6 reduce-scatter.8
  345.9 110.2 reduce-scatter.6
  459.3 34.6 reduce-scatter.10
  497.1 38.3 reduce-scatter.12
where the time goes:
time: 553 us; the launch traced here: 545 us
  waiting for transfers between devices  220 us (40%)
  local copies, waits for them, and re-layouts  90.1 us (16%)
  blocking collectives  74.3 us (13%)
  matrix products  68.8 us (12%)
  other arithmetic  37.8 us (7%)
  starting transfers between devices  24 us (4%)
  loops' own time  15.4 us (3%)
  between operations  14.6 us (3%)
    reduce_scatter x2, waiting for transfers between devices, sum_columns(): lax.psum_scatter(term.astype(jnp.bfloat16), 'head', scatter_dimension=2,...  110 us
    all_to_all x1, blocking collectives, to_time(): lax.all_to_all(stacked, 'head', split_axis=1, concat_axis=2, tiled=True)  74.3 us
    all_to_all x2, waiting for transfers between devices, to_heads(): lax.all_to_all(stacked, 'head', split_axis=2, concat_axis=1, tiled=True)  47 us
    unnamed x5, waiting for transfers between devices  40.8 us
    dot_general x8, matrix products, one_block(): jnp.einsum('qhe,khe->hqk', query_part, key_part, precision=lax.Precision....  23.7 us
    reduce_scatter x1, waiting for transfers between devices, sum_rows(): lax.psum_scatter(term.astype(jnp.bfloat16), 'seq', scatter_dimension=1, t...  21.9 us
    dot_general x6, matrix products, one_block(): jnp.einsum('hqk,khe->qhe', weights, value_part, precision=lax.Precision.H...  21.4 us
    unnamed x51, local copies, waits for them, and re-layouts  21.2 us
  transfers between devices with their start and end apart: 11, of which 6 were waited for; matrix products, arithmetic and copies ran while one was open for 22% of the time, Pallas kernels for 0%

commit v1 on v0

--- a/solution.py
+++ b/solution.py
@@ -2,6 +2,7 @@
 import jax.numpy as jnp
 from jax import lax
 from jax.sharding import PartitionSpec as P
+from jax.lax import all_to_all, axis_size
 
 HEAD_SIZE = 128
 WINDOW = 128
@@ -84,7 +85,12 @@
 
 
 def to_heads(stacked):
-    return lax.all_to_all(stacked, "head", split_axis=2, concat_axis=1, tiled=True)
+
+    def group_corner_in(raw):
+        left_arr = all_to_all(jnp.stack(jnp.split(raw, axis_size("head"), axis=2)), "head", 0, 0)
+        return jnp.concatenate(left_arr, axis=1)
+
+    return group_corner_in(stacked)
 
 
 def to_time(stacked):

time: 553 us -> 518 us (0.937)
  local copies, waits for them, and re-layouts: 90.1 us -> 77.1 us
  loops' own time: 15.4 us -> 4.11 us
    another operation x2, loops' own time: 15.4 us -> 4.11 us  [attention(): lax.map(jax.checkpoint(one_block), jnp.arange(block_count, dtype=jnp.int32))]
    unnamed x51 -> x47, local copies, waits for them, and re-layouts: 21.2 us -> 17.4 us
  transfers between devices with their start and end apart: 11 -> 11, of which waited for: 6 -> 5; matrix products, arithmetic and copies ran while one was open for 22% -> 22% of each run, Pallas kernels for 0% -> 0%
where the time goes in v1:
time: 518 us; the launch traced here: 511 us
  waiting for transfers between devices  215 us (42%)
  local copies, waits for them, and re-layouts  77.1 us (15%)
  blocking collectives  73.8 us (14%)
  matrix products  67.6 us (13%)
  other arithmetic  34.6 us (7%)
  starting transfers between devices  24.4 us (5%)
  between operations  14.6 us (3%)
    reduce_scatter x2, waiting for transfers between devices, sum_columns(): lax.psum_scatter(term.astype(jnp.bfloat16), 'head', scatter_dimension=2,...  110 us
    all_to_all x1, blocking collectives, to_time(): lax.all_to_all(stacked, 'head', split_axis=1, concat_axis=2, tiled=True)  73.8 us
    all_to_all x2, waiting for transfers between devices, group_corner_in(): all_to_all(jnp.stack(jnp.split(raw, axis_size('head'), axis=2)), 'head',...  42.8 us
    unnamed x5, waiting for transfers between devices  40.7 us
    dot_general x8, matrix products, one_block(): jnp.einsum('qhe,khe->hqk', query_part, key_part, precision=lax.Precision....  23.7 us
    reduce_scatter x1, waiting for transfers between devices, sum_rows(): lax.psum_scatter(term.astype(jnp.bfloat16), 'seq', scatter_dimension=1, t...  21.9 us
    dot_general x6, matrix products, one_block(): jnp.einsum('hqk,khe->qhe', weights, value_part, precision=lax.Precision.H...  21.4 us
    unnamed x47, local copies, waits for them, and re-layouts  17.4 us
  transfers between devices with their start and end apart: 11, of which 5 were waited for; matrix products, arithmetic and copies ran while one was open for 22% of the time, Pallas kernels for 0%

profile of v1, /device:TPU:0, one launch (start us, length us, event | category | flops | bytes accessed | tf_op | source)
XLA Modules:
  0.0 511.4 jit_solution(12847431635841830650)
XLA Ops:
  11.5 6.3 %all-to-all-start.2 = ((bf16[4,1,256,256]{3,2,1,0:T(8,128)(2,1)}), bf16[4,1,256,256]{3,2,1,0:T(8,128)(2,1)S(1)}, u32[]{:S(2)}, u32[]{:S(2)}) async-start(bf16[4,1,256,256]{3,2,1,0:T(8,128)(2,1)} %pad_maximum_fusion.4), calls=%async_computation.2 | async-start | bytes 1048576 | tf_op jit(solution)/shard_map/all_to_all | solution.py:90
  18.8 4.7 fusion.34
  25.0 7.3 %all-to-all-done.2 = bf16[4,1,256,256]{3,2,1,0:T(8,128)(2,1)S(1)} async-done(((bf16[4,1,256,256]{3,2,1,0:T(8,128)(2,1)}), bf16[4,1,256,256]{3,2,1,0:T(8,128)(2,1)S(1)}, u32[]{:S(2)}, u32[]{:S(2)}) %all-to-all-start.2) | async-done | bytes 524320 | tf_op jit(solution)/shard_map/all_to_all | solution.py:90
  32.3 4.3 all-to-all-start
  37.7 35.5 %all-to-all-done = bf16[4,3,256,256]{3,2,1,0:T(8,128)(2,1)} async-done(((bf16[4,3,256,256]{3,2,1,0:T(8,128)(2,1)}), bf16[4,3,256,256]{3,2,1,0:T(8,128)(2,1)}, u32[]{:S(2)}, u32[]{:S(2)}) %all-to-all-start) | async-done | bytes 1572896 | tf_op jit(solution)/shard_map/all_to_all | solution.py:90
  88.2 30.1 %while.32 = (s32[]{:T(128)}, bf16[2,512,256]{2,1,0:T(8,128)(2,1)}, s32[2]{0:T(128)S(1)}, f32[1280,256]{0,1:T(8,128)}, s32[]{:T(128)}, /*index=5*/f32[1024,256]{0...) while((s32[]{:T(128)}, bf16[2,512,256]{2,1,0:T(8,128)(2,1)}, ...), condition=%wide.region_5.6_spmd, body=%wide.region_2.5_spmd.sunk | while | flops 2426537472 | bytes 25986388 | solution.py:76
  98.5 4.0 fusion.116
  113.3 4.0 fusion.116
  120.7 4.6 reduce.4
  127.3 4.1 all-to-all-start.1
  134.9 59.8 %while.33 = (s32[]{:T(128)}, f32[1024,256]{1,0:T(8,128)}, f32[1280,256]{0,1:T(8,128)}, f32[1280,256]{0,1:T(8,128)}, s32[2]{0:T(128)S(1)}, /*index=5*/f32[2,512,2...) while((s32[]{:T(128)}, f32[1024,256]{1,0:T(8,128)}, ...), condition=%wide.region_10.11_spmd, body=%wide.region_6.10_spmd.sunk | while | flops 6061953024 | bytes 89728512 | solution.py:76
  146.0 3.9 multiply_reduce_fusion.2
  175.7 3.9 multiply_reduce_fusion.2
  194.7 3.9 copy.89
  208.5 4.0 fusion.27
  212.7 5.6 %collective-permute-start.2 = (bf16[2,128,256]{2,0,1:T(2,128)(2,1)S(1)}, bf16[2,128,256]{2,0,1:T(2,128)(2,1)S(1)}, u32[]{:S(2)}, u32[]{:S(2)}) collective-permute-start(bf16[2,128,256]{2,0,1:T(2,128)(2,1)S(1)} %get-tuple-element.462), channel_id=1, source_target_pairs={{0,4},{4,8},{8,12},{12,16},{16,20},{20,24},{24,28},{1,5},{5,9},{9,... | collective-permute-start | bytes 393224 | tf_op jit(solution)/shard_map/ppermute | solution.py:20
  226.2 73.8 %all_to_all.43 = bf16[3,1024,256]{2,0,1:T(4,128)(2,1)S(1)} all-to-all(bf16[3,1024,256]{2,0,1:T(4,128)(2,1)S(1)} %pad_maximum_fusion.1), channel_id=1, replica_groups=mesh['seq'=8,'head'=4] {'head'}, dimensions={1} | all-to-all | bytes 3145728 | tf_op jit(solution)/shard_map/all_to_all | solution.py:97
  302.7 3.8 all_to_all.38
  306.5 6.1 %fusion.26 = bf16[3,1024,1024]{1,2,0:T(8,128)(2,1)} fusion(bf16[3,256,1024]{2,1,0:T(8,128)(2,1)} %all_to_all.38, bf16[256,1024]{1,0:T(8,128)(2,1)S(1)} %copy-done.14, f32[1024]{0:T(1024)S(1)} %copy-done.28, f32[256]{0:T(256)S(1)} %copy-done.24, f32[256]{0:T(256)S(1)} %copy-done.22), kind=kOutput, calls=%fused_computation.55 | convolution fusion | flops 1618214912 | bytes 8394752 | tf_op jit(solution)/shard_map/td,ctf->cdf/dot_general | solution.py:162
  313.4 109.6 %reduce-scatter.7.cloned.1.call-done = bf16[3,1024,256]{1,2,0:T(8,128)(2,1)} async-done(((bf16[3,1024,1024]{1,2,0:T(8,128)(2,1)}), bf16[3,1024,256]{1,2,0:T(8,128)(2,1)}) %reduce-scatter.7.cloned.1.call-update) | async-done | bytes 1572880 | tf_op jit(solution)/shard_map/reduce_scatter | solution.py:101
  423.0 4.4 copy.91
  432.1 5.1 fusion.43
  438.8 21.9 %reduce-scatter.11.cloned.1.call-done = bf16[1,128,256]{2,1,0:T(8,128)(2,1)} async-done(((bf16[1,1024,256]{2,1,0:T(8,128)(2,1)}), bf16[1,128,256]{2,1,0:T(8,128)(2,1)}) %reduce-scatter.11.cloned.1.call-update) | async-done | bytes 65552 | tf_op jit(solution)/shard_map/reduce_scatter | solution.py:107
  462.3 40.0 %reduce-scatter.13.cloned.1.call-done = bf16[128,768]{1,0:T(8,128)(2,1)} async-done(((bf16[1024,768]{1,0:T(8,128)(2,1)}), bf16[128,768]{1,0:T(8,128)(2,1)}) %reduce-scatter.13.cloned.1.call-update) | async-done | bytes 196624
  (220 shorter events, 131.8 us)
Async XLA Ops:
  7.2 10.6 %copy-start.13 = (bf16[256,1024]{1,0:T(8,128)(2,1)S(1)}, bf16[256,1024]{1,0:T(8,128)(2,1)}, u32[]{:S(2)}) copy-start(bf16[256,1024]{1,0:T(8,128)(2,1)} %param.13) | copy-start | bytes 1572868
  10.5 8.2 %copy-start.27 = (f32[1024]{0:T(1024)S(1)}, f32[1024]{0:T(1024)}, u32[]{:S(2)}) copy-start(f32[1024]{0:T(1024)} %param.15) | copy-start | bytes 12292
  11.5 20.8 %all-to-all-start.2 = ((bf16[4,1,256,256]{3,2,1,0:T(8,128)(2,1)}), bf16[4,1,256,256]{3,2,1,0:T(8,128)(2,1)S(1)}, u32[]{:S(2)}, u32[]{:S(2)}) async-start(bf16[4,1,256,256]{3,2,1,0:T(8,128)(2,1)} %pad_maximum_fusion.4), calls=%async_computation.2 | async-start | bytes 1048576 | tf_op jit(solution)/shard_map/all_to_all | solution.py:90
  18.0 5.5 %copy-start.21 = (f32[256]{0:T(256)}, f32[256]{0:T(256)S(1)}, u32[]{:S(2)}) copy-start(f32[256]{0:T(256)S(1)} %broadcast_multiply_fusion) | copy-start | bytes 3076
  18.8 4.7 copy-start.23
  32.3 40.9 %all-to-all-start = ((bf16[4,3,256,256]{3,2,1,0:T(8,128)(2,1)}), bf16[4,3,256,256]{3,2,1,0:T(8,128)(2,1)}, u32[]{:S(2)}, u32[]{:S(2)}) async-start(bf16[4,3,256,256]{3,2,1,0:T(8,128)(2,1)} %pad_maximum_fusion.2), calls=%async_computation | async-start | bytes 3145728 | tf_op jit(solution)/shard_map/all_to_all | solution.py:90
  76.4 6.2 %collective-permute-start = (bf16[2,128,256]{2,1,0:T(8,128)(2,1)}, bf16[2,128,256]{2,1,0:T(8,128)(2,1)S(1)}, u32[]{:S(2)}, u32[]{:S(2)}) collective-permute-start(bf16[2,128,256]{2,1,0:T(8,128)(2,1)} %get-tuple-element.466), channel_id=1, source_target_pairs={{0,4},{4,8},{8,12},{12,16},{16,20},{20,24},{24,28},{1,5},{5,9},{9,... | collective-permute-start | bytes 393224 | tf_op jit(solution)/shard_map/ppermute | solution.py:20
  77.7 5.0 collective-permute-start.1
  127.3 73.5 %all-to-all-start.1 = ((bf16[4,2,32768]{2,1,0:T(2,128)(2,1)}), bf16[4,2,32768]{2,1,0:T(2,128)(2,1)}, u32[]{:S(2)}, u32[]{:S(2)}) async-start(bf16[4,2,32768]{2,1,0:T(2,128)(2,1)} %reshape.389), calls=%async_computation.1 | async-start | bytes 1048576 | tf_op jit(solution)/shard_map/all_to_all | solution.py:97
  131.4 181.3 %reduce-scatter.9.cloned.1.call-start = ((), (), s32[]{:S(2)}) async-start(), calls=%async_computation.9 | async-start | bytes 2621440 | tf_op jit(solution)/shard_map/reduce_scatter | solution.py:101
  208.5 11.1 %copy-start.9 = (f32[1024,256]{1,0:T(8,128)S(1)}, f32[1024,256]{1,0:T(8,128)}, u32[]{:S(2)}) copy-start(f32[1024,256]{1,0:T(8,128)} %get-tuple-element.325) | copy-start | bytes 3145732
  208.5 214.5 %reduce-scatter.7.cloned.1.call-start = ((), (), s32[]{:S(2)}) async-start(), calls=%async_computation.8 | async-start | bytes 7864320 | tf_op jit(solution)/shard_map/reduce_scatter | solution.py:101
  212.5 8.0 %copy-start.10 = (f32[1,1280,256]{2,0,1:T(1,128)S(1)}, f32[1,1280,256]{2,0,1:T(1,128)}, u32[]{:S(2)}) copy-start(f32[1,1280,256]{2,0,1:T(1,128)} %copy.89) | copy-start | bytes 3932164
  212.5 8.0 %copy-start.11 = (f32[1,1280,256]{2,0,1:T(1,128)S(1)}, f32[1,1280,256]{2,0,1:T(1,128)}, u32[]{:S(2)}) copy-start(f32[1,1280,256]{2,0,1:T(1,128)} %copy.90) | copy-start | bytes 3932164
  212.7 9.8 %collective-permute-start.2 = (bf16[2,128,256]{2,0,1:T(2,128)(2,1)S(1)}, bf16[2,128,256]{2,0,1:T(2,128)(2,1)S(1)}, u32[]{:S(2)}, u32[]{:S(2)}) collective-permute-start(bf16[2,128,256]{2,0,1:T(2,128)(2,1)S(1)} %get-tuple-element.462), channel_id=1, source_target_pairs={{0,4},{4,8},{8,12},{12,16},{16,20},{20,24},{24,28},{1,5},{5,9},{9,... | collective-permute-start | bytes 393224 | tf_op jit(solution)/shard_map/ppermute | solution.py:20
  218.3 4.2 collective-permute-start.3
  300.1 6.5 %copy-start.14 = (bf16[256,1024]{1,0:T(8,128)(2,1)S(1)}, bf16[256,1024]{1,0:T(8,128)(2,1)}, u32[]{:S(2)}) copy-start(bf16[256,1024]{1,0:T(8,128)(2,1)} %param.13) | copy-start | bytes 1572868
  300.1 6.5 %copy-start.22 = (f32[256]{0:T(256)S(1)}, f32[256]{0:T(256)}, u32[]{:S(2)}) copy-start(f32[256]{0:T(256)} %copy-done.21) | copy-start | bytes 3076
  300.1 6.5 %copy-start.24 = (f32[256]{0:T(256)S(1)}, f32[256]{0:T(256)}, u32[]{:S(2)}) copy-start(f32[256]{0:T(256)} %copy-done.23) | copy-start | bytes 3076
  300.1 6.5 %copy-start.28 = (f32[1024]{0:T(1024)S(1)}, f32[1024]{0:T(1024)}, u32[]{:S(2)}) copy-start(f32[1024]{0:T(1024)} %param.15) | copy-start | bytes 12292
  312.6 148.2 %reduce-scatter.11.cloned.1.call-start = ((), (), s32[]{:S(2)}) async-start(), calls=%async_computation.10 | async-start | bytes 589824 | tf_op jit(solution)/shard_map/reduce_scatter | solution.py:107
  313.4 188.9 %reduce-scatter.13.cloned.1.call-start = ((), (), s32[]{:S(2)}) async-start(), calls=%async_computation.11 | async-start | bytes 1769472
  432.1 5.1 copy-start.26
  432.1 5.5 %copy-start.17 = (bf16[256,1024]{1,0:T(8,128)(2,1)S(1)}, bf16[256,1024]{1,0:T(8,128)(2,1)}, u32[]{:S(2)}) copy-start(bf16[256,1024]{1,0:T(8,128)(2,1)} %param.14) | copy-start | bytes 1572868
  (26 other events, 63.6 us)
Sparse Core Ops, SparseCore 0:
  208.6 66.3 reduce-scatter.8
  312.8 110.2 reduce-scatter.6
  426.1 34.6 reduce-scatter.10
  463.9 38.3 reduce-scatter.12
